TPU v7x, 256 devices: a whole 4x4x8 slice. The times are simulated.
256 devices in a mesh: rows: 8 (over z), cols: 32 (over y, x, core).
Axes of the slice: x: 4, y: 4, z: 8, core: 2. Of those that a mesh axis runs over, the one named last changes fastest.
Arguments:
- whitened: float32 [3, 1048576], P(None, ('rows', 'cols')), may hold values from -6 to 6
- cotangent: bfloat16 [64, 1048576], P(None, ('rows', 'cols')), may hold values from -6 to 6
- lift_weight: float32 [64, 3], replicated, may hold values from -3.5 to 3.5
- conv_now: bfloat16 [3, 128, 64], replicated, may hold values from -0.5 to 0.5
- conv_past: bfloat16 [3, 128, 64], replicated, may hold values from -0.5 to 0.5
- mix_weight: bfloat16 [3, 64, 64], replicated, may hold values from -0.75 to 0.75
- dilations: int32 [3], replicated, may hold values from 64 to 256, as said below
- psd_bin: int32 [4096, 32, 8], P(None, 'cols', 'rows'), may hold values from 0 to 1023, as said below
- psd_weight: float32 [2, 1024], replicated, may hold values from 0.2 to 5
Outputs:
- data_grad: float32 [3, 1048576], P(None, ('rows', 'cols'))
- grad_now: float32 [3, 128, 64], replicated
- grad_past: float32 [3, 128, 64], replicated
- grad_mix: float32 [3, 64, 64], replicated
- grad_lift: float32 [64, 3], replicated
Inputs may be any that keep to these rules, and one draw needn't show every extreme that they name: `dilations`: multiples of 4; one layer has 64, one has 256. `psd_bin`: frequencies k and 1048576 - k have the same bin.
All inputs are finite; a program needn't handle non-finite values.
Results may differ from a plain program's by a relative error of at most 0.0068.
Values may be sent and summed in bfloat16 or wider, within the bound.
No kernel may reach another device: no remote copies, remote signals or barrier semaphores. Data moves between devices by JAX's collectives and lax.ppermute only.
A program may use at most 64 MiB of HBM per device.

v0:
```python
import math
import jax
import jax.numpy as jnp
from jax import lax
from jax.sharding import PartitionSpec as P

DMAX = 256


def from_behind(array, axis, by):
    peers = lax.axis_size(axis)
    pairs = [(i, i + by) for i in range(peers) if 0 <= i + by < peers]
    return lax.ppermute(array, axis, pairs)


def lifted(lift_weight, inputs):
    return (
        lift_weight[:, 0:1] * inputs[0:1]
        + lift_weight[:, 1:2] * inputs[1:2]
        + lift_weight[:, 2:3] * inputs[2:3]
    )


def delayed(field_b, delay, before):
    joined = jnp.concatenate([before, field_b], axis=1)
    start_at = before.shape[1] - delay
    return lax.dynamic_slice_in_dim(joined, start_at, field_b.shape[1], 1)


def advanced(values, delay, head_rim):
    joined = jnp.concatenate([values, head_rim], axis=1)
    return lax.dynamic_slice_in_dim(joined, delay, values.shape[1], 1)


def gated_layer(field_now, field_b, before, weight_now, weight_past, weight_mix, delay):
    channel_count = weight_mix.shape[0]
    past_b = delayed(field_b, delay, before)
    pre_act = jnp.dot(weight_now, field_b, preferred_element_type=jnp.float32) + jnp.dot(
        weight_past, past_b, preferred_element_type=jnp.float32
    )
    tanh_part = jnp.tanh(pre_act[:channel_count])
    sigm_part = jax.nn.sigmoid(pre_act[channel_count:])
    gate_b = (tanh_part * sigm_part).astype(jnp.bfloat16)
    field_next = field_now + jnp.dot(weight_mix, gate_b, preferred_element_type=jnp.float32)
    return (field_next, (field_b, past_b, tanh_part, sigm_part, gate_b))


def phase_angle(product, modulus, sign_factor):
    return sign_factor * 2.0 * math.pi / modulus * (product % modulus).astype(jnp.float32)


def phase_table(modulus, sign_factor):
    ordinal = jnp.arange(modulus, dtype=jnp.int32)
    angles = phase_angle(ordinal[:, None] * ordinal[None, :], modulus, sign_factor)
    return (jnp.cos(angles), jnp.sin(angles))


def rotate(signals, angles):
    real_part, imag_part = signals
    cosine = jnp.cos(angles)
    sine_part = jnp.sin(angles)
    return (real_part * cosine - imag_part * sine_part, real_part * sine_part + imag_part * cosine)


def transform(pattern, table_pair, signals):
    cosine, sine_part = table_pair
    real_part, imag_part = signals
    first_term = jnp.einsum(pattern, cosine, real_part, precision=lax.Precision.HIGHEST)
    second = jnp.einsum(pattern, sine_part, real_part, precision=lax.Precision.HIGHEST)
    if imag_part is None:
        return (first_term, second)
    return (
        first_term - jnp.einsum(pattern, sine_part, imag_part, precision=lax.Precision.HIGHEST),
        second + jnp.einsum(pattern, cosine, imag_part, precision=lax.Precision.HIGHEST),
    )


def split_length(length_all):
    chosen = 1
    for factor in range(1, length_all + 1):
        if length_all % factor == 0 and factor * factor <= length_all:
            chosen = factor
    return (chosen, length_all // chosen)


def pair_up(moved):
    return ((moved, None), (0, 0, 1))


def local_section(signals, psd_bin, psd_weight, weight_rows):
    rows_count = lax.axis_size("rows")
    row_index = lax.axis_index("rows")
    col_index = lax.axis_index("cols")
    signal_count = len(weight_rows)
    segment = signals[0].shape[1]
    length_all = segment * rows_count * lax.axis_size("cols")
    slow_len, fast_len = split_length(segment)
    slow_ids = jnp.arange(slow_len, dtype=jnp.int32)
    fast_ids = jnp.arange(fast_len, dtype=jnp.int32)
    spectra = (
        signals[0].reshape(signal_count, slow_len, fast_len),
        signals[1].reshape(signal_count, slow_len, fast_len),
    )
    spectra = transform("pa,kpq->kaq", phase_table(slow_len, -1.0), spectra)
    spectra = rotate(
        spectra, phase_angle(slow_ids[:, None] * fast_ids[None, :], segment, -1.0)[None]
    )
    spectra = transform("qb,kaq->kab", phase_table(fast_len, -1.0), spectra)
    bins_here = psd_bin.reshape(fast_len, slow_len).T
    weights = jnp.take(psd_weight, bins_here, axis=1)
    factors = jnp.stack([weights[row_id] for row_id in weight_rows])
    spectra = (spectra[0] * factors, spectra[1] * factors)
    spectra = transform("bq,kab->kaq", phase_table(fast_len, 1.0), spectra)
    spectra = rotate(
        spectra, phase_angle(slow_ids[:, None] * fast_ids[None, :], segment, 1.0)[None]
    )
    spectra = transform("ap,kaq->kpq", phase_table(slow_len, 1.0), spectra)
    low_here = row_index + rows_count * col_index
    sample_all = jnp.arange(segment, dtype=jnp.int32)
    return rotate(
        (spectra[0].reshape(signal_count, segment), spectra[1].reshape(signal_count, segment)),
        phase_angle(sample_all * low_here, length_all, 1.0)[None],
    )


def per_axis_filter(signal, psd_bin, psd_weight):
    rows_count = lax.axis_size("rows")
    cols_count = lax.axis_size("cols")
    row_index = lax.axis_index("rows")
    col_index = lax.axis_index("cols")
    segment = signal.shape[1]
    groups = rows_count * cols_count
    length_all = segment * groups
    piece_len = segment // rows_count
    small_len = segment // groups
    outer_ids = jnp.arange(rows_count, dtype=jnp.int32)
    inner_ids = jnp.arange(cols_count, dtype=jnp.int32)
    moved = lax.all_to_all(
        signal.reshape(3, 1, segment), "rows", split_axis=2, concat_axis=1, tiled=True
    )
    signals, weight_rows = pair_up(moved)
    signal_count = len(weight_rows)
    signals = transform("ra,krj->kaj", phase_table(rows_count, -1.0), signals)
    signals = rotate(signals, phase_angle(col_index * outer_ids, groups, -1.0)[None, :, None])
    pieces = (
        lax.all_to_all(
            signals[0].reshape(signal_count, rows_count, 1, piece_len),
            "cols",
            split_axis=3,
            concat_axis=2,
            tiled=True,
        ),
        lax.all_to_all(
            signals[1].reshape(signal_count, rows_count, 1, piece_len),
            "cols",
            split_axis=3,
            concat_axis=2,
            tiled=True,
        ),
    )
    turned = transform("cb,kacm->kabm", phase_table(cols_count, -1.0), (pieces[0], pieces[1]))
    freq_low = outer_ids[:, None, None] + rows_count * inner_ids[None, :, None]
    sample_at = (
        row_index * piece_len
        + col_index * small_len
        + jnp.arange(small_len, dtype=jnp.int32)[None, None, :]
    )
    turned = rotate(turned, phase_angle(sample_at * freq_low, length_all, -1.0)[None])
    signals = (
        lax.all_to_all(turned[0], "cols", split_axis=2, concat_axis=3, tiled=True),
        lax.all_to_all(turned[1], "cols", split_axis=2, concat_axis=3, tiled=True),
    )
    signals = (
        lax.all_to_all(
            signals[0].reshape(signal_count, rows_count, piece_len),
            "rows",
            split_axis=1,
            concat_axis=2,
            tiled=True,
        ),
        lax.all_to_all(
            signals[1].reshape(signal_count, rows_count, piece_len),
            "rows",
            split_axis=1,
            concat_axis=2,
            tiled=True,
        ),
    )
    flat = local_section(
        (signals[0].reshape(signal_count, segment), signals[1].reshape(signal_count, segment)),
        psd_bin,
        psd_weight,
        weight_rows,
    )
    returned = (
        lax.all_to_all(
            flat[0].reshape(signal_count, 1, segment),
            "rows",
            split_axis=2,
            concat_axis=1,
            tiled=True,
        ),
        lax.all_to_all(
            flat[1].reshape(signal_count, 1, segment),
            "rows",
            split_axis=2,
            concat_axis=1,
            tiled=True,
        ),
    )
    pieces = (
        lax.all_to_all(
            returned[0].reshape(signal_count, rows_count, 1, piece_len),
            "cols",
            split_axis=3,
            concat_axis=2,
            tiled=True,
        ),
        lax.all_to_all(
            returned[1].reshape(signal_count, rows_count, 1, piece_len),
            "cols",
            split_axis=3,
            concat_axis=2,
            tiled=True,
        ),
    )
    turned = transform("bc,kabm->kacm", phase_table(cols_count, 1.0), (pieces[0], pieces[1]))
    turned = rotate(
        turned, phase_angle(inner_ids[None, :, None] * outer_ids[:, None, None], groups, 1.0)[None]
    )
    returned = (
        lax.all_to_all(turned[0], "cols", split_axis=2, concat_axis=3, tiled=True),
        lax.all_to_all(turned[1], "cols", split_axis=2, concat_axis=3, tiled=True),
    )
    real_in = returned[0].reshape(signal_count, rows_count, piece_len)
    imag_in = returned[1].reshape(signal_count, rows_count, piece_len)
    cos_rows, sin_rows = phase_table(rows_count, 1.0)
    real_out = jnp.einsum(
        "ar,kaj->krj", cos_rows, real_in, precision=lax.Precision.HIGHEST
    ) - jnp.einsum("ar,kaj->krj", sin_rows, imag_in, precision=lax.Precision.HIGHEST)
    homed = lax.all_to_all(real_out, "rows", split_axis=1, concat_axis=2, tiled=True)
    return homed.reshape(3, segment) / float(length_all)


def local(
    whitened,
    cotangent,
    lift_weight,
    conv_now,
    conv_past,
    mix_weight,
    dilations,
    psd_bin,
    psd_weight,
):
    segment = whitened.shape[1]
    layer_count = mix_weight.shape[0]
    saved = []
    field_now = lifted(lift_weight, whitened)
    for layer_id in range(layer_count):
        field_b = field_now.astype(jnp.bfloat16)
        before = from_behind(field_b[:, segment - DMAX :], ("rows", "cols"), 1)
        field_now, kept_parts = gated_layer(
            field_now,
            field_b,
            before,
            conv_now[layer_id],
            conv_past[layer_id],
            mix_weight[layer_id],
            dilations[layer_id],
        )
        saved.append(kept_parts)
    grad_field = cotangent.astype(jnp.float32)
    grads_now = [None] * layer_count
    grads_past = [None] * layer_count
    grads_mix = [None] * layer_count
    for layer_id in reversed(range(layer_count)):
        field_b, past_b, tanh_part, sigm_part, gate_b = saved[layer_id]
        grad_field_b = grad_field.astype(jnp.bfloat16)
        grad_gate = jnp.dot(
            mix_weight[layer_id].T, grad_field_b, preferred_element_type=jnp.float32
        )
        grads_mix[layer_id] = jnp.dot(grad_field_b, gate_b.T, preferred_element_type=jnp.float32)
        grad_pre = jnp.concatenate(
            [
                grad_gate * sigm_part * (1.0 - tanh_part * tanh_part),
                grad_gate * tanh_part * sigm_part * (1.0 - sigm_part),
            ],
            axis=0,
        ).astype(jnp.bfloat16)
        grads_now[layer_id] = jnp.dot(grad_pre, field_b.T, preferred_element_type=jnp.float32)
        grads_past[layer_id] = jnp.dot(grad_pre, past_b.T, preferred_element_type=jnp.float32)
        ahead_term = jnp.dot(conv_past[layer_id].T, grad_pre, preferred_element_type=jnp.float32)
        head_rim = from_behind(ahead_term[:, :DMAX], ("rows", "cols"), -1)
        grad_field = (
            grad_field
            + jnp.dot(conv_now[layer_id].T, grad_pre, preferred_element_type=jnp.float32)
            + advanced(ahead_term, dilations[layer_id], head_rim)
        )
    input_grad = jnp.dot(lift_weight.T, grad_field, precision=lax.Precision.HIGHEST)
    lift_part = jnp.dot(grad_field, whitened.T, precision=lax.Precision.HIGHEST)
    summed = lax.psum(
        (jnp.stack(grads_now), jnp.stack(grads_past), jnp.stack(grads_mix), lift_part),
        ("rows", "cols"),
    )
    scaling = 1.0 / math.sqrt(float(segment * lax.axis_size("rows") * lax.axis_size("cols")))
    data_grad = per_axis_filter(input_grad, psd_bin, psd_weight)
    return (
        data_grad,
        summed[0] * scaling,
        summed[1] * scaling,
        summed[2] * scaling,
        summed[3] * scaling,
    )


def solution(mesh):
    in_specs = (
        P(None, ("rows", "cols")),
        P(None, ("rows", "cols")),
        P(),
        P(),
        P(),
        P(),
        P(),
        P(None, "cols", "rows"),
        P(),
    )
    out_specs = (P(None, ("rows", "cols")), P(), P(), P(), P())
    return jax.shard_map(local, mesh=mesh, in_specs=in_specs, out_specs=out_specs, check_vma=False)
```

profile of v0, /device:TPU:1, one launch (start us, length us, event | category | flops | bytes accessed | tf_op | source)
XLA Modules:
  0.0 555.5 jit_solution(1703089150025152943)
XLA Ops:
  9.3 4.6 collective-permute-start
  21.3 10.8 %gather_fusion = f32[4096,2]{1,0:T(8,128)S(1)} fusion(f32[2,1024]{0,1:T(8,128)S(1)} %copy.178, s32[4096]{0:T(1024)S(1)} %broadcast_clamp_fusion), kind=kCustom, calls=%fused_computation | custom fusion | bytes 81920 | tf_op jit(solution)/shard_map/jit(_take)/gather | solution.py:110
  48.6 1.9 collective-permute-start.1
  53.0 4.1 collective-permute-start.2
  60.9 1.9 collective-permute-start.3
  63.9 3.1 collective-permute-done.3
  68.8 2.1 collective-permute-start.4
  72.1 2.3 collective-permute-done.4
  76.1 1.9 collective-permute-start.5
  79.2 2.5 collective-permute-done.5
  83.1 3.7 copy.151
  87.3 20.4 %reduce.4 = f32[4096,3]{1,0:T(8,128)} reduce(f32[4096,1,3]{2,1,0:T(1,128)} %bitcast.335, f32[]{:T(128)} %broadcast.734), dimensions={1}, to_apply=%bitcast.265.reduce_sub_computation | reduce | bytes 98308
  107.7 3.7 reshape.486
  111.4 21.0 %all-to-all-start = ((f32[8,1,1536]{2,1,0:T(1,128)}), f32[8,1,1536]{2,1,0:T(1,128)S(1)}, u32[]{:S(2)}, u32[]{:S(2)}) async-start(f32[8,1,1536]{2,1,0:T(1,128)} %reshape.486), calls=%async_computation | async-start | bytes 98304 | tf_op jit(solution)/shard_map/all_to_all | solution.py:138
  132.5 1.9 convolution_bitcast_fusion.18
  134.4 5.1 all-to-all-done
  140.3 4.4 reshape.487
  144.7 2.2 copy.231
  148.0 2.0 copy.153
  150.0 4.2 reduce.6
  154.2 2.5 reshape.488
  156.7 14.5 %all-to-all-start.1 = ((f32[32,1,384]{2,1,0:T(1,128)}), f32[32,1,384]{2,1,0:T(1,128)S(1)}, u32[]{:S(2)}, u32[]{:S(2)}) async-start(f32[32,1,384]{2,1,0:T(1,128)} %reshape.488), calls=%async_computation.1 | async-start | bytes 98304 | tf_op jit(solution)/shard_map/all_to_all | solution.py:146
  171.2 2.4 convolution_bitcast_fusion.12
  173.5 1.7 copy.156
  175.3 4.0 reduce.8
  180.5 7.9 %all-to-all-start.2 = ((f32[32,1,384]{2,1,0:T(1,128)}), f32[32,1,384]{2,1,0:T(1,128)S(1)}, u32[]{:S(2)}, u32[]{:S(2)}) async-start(f32[32,1,384]{2,1,0:T(1,128)} %reshape.490), calls=%async_computation.2 | async-start | bytes 98304 | tf_op jit(solution)/shard_map/all_to_all | solution.py:153
  197.6 1.8 copy.157
  200.3 1.7 fusion.12
  202.1 2.4 multiply_add_fusion.1
  206.4 6.2 %all-to-all-start.3 = ((f32[32,1,384]{2,1,0:T(1,128)}), f32[32,1,384]{2,1,0:T(1,128)}, u32[]{:S(2)}, u32[]{:S(2)}) async-start(f32[32,1,384]{2,1,0:T(1,128)} %reshape.492), calls=%async_computation.3 | async-start | bytes 98304 | tf_op jit(solution)/shard_map/all_to_all | solution.py:170
  212.7 2.2 convolution_bitcast_fusion.16
  215.9 4.1 all-to-all-done.3
  220.0 4.5 all-to-all-start.5
  225.4 1.6 reduce.10
  228.2 3.8 all-to-all-done.5
  232.0 3.4 all-to-all-start.4
  240.1 2.3 all-to-all-done.4
  242.4 4.5 all-to-all-start.6
  247.8 6.3 %all-to-all-done.6 = f32[3,8,512]{2,0,1:T(4,128)S(1)} async-done(((f32[3,8,512]{2,0,1:T(4,128)}), f32[3,8,512]{2,0,1:T(4,128)S(1)}, u32[]{:S(2)}, u32[]{:S(2)}) %all-to-all-start.6) | async-done | bytes 49184 | tf_op jit(solution)/shard_map/all_to_all | solution.py:181
  260.1 2.4 copy.188
  262.5 19.4 %reduce.12 = f32[4096,3]{1,0:T(8,128)} reduce(f32[4096,1,3]{2,1,0:T(1,128)S(1)} %bitcast.337, f32[]{:T(128)} %broadcast.734), dimensions={1}, to_apply=%bitcast.275.reduce_sub_computation | reduce | bytes 98308
  281.9 3.7 reshape.496
  285.6 3.3 all-to-all-start.7
  289.9 2.4 copy.193
  292.4 19.4 %reduce.16 = f32[4096,3]{1,0:T(8,128)} reduce(f32[4096,1,3]{2,1,0:T(1,128)S(1)} %bitcast.338, f32[]{:T(128)} %broadcast.734), dimensions={1}, to_apply=%bitcast.279.reduce_sub_computation | reduce | bytes 98308
  311.8 3.7 reshape.500
  315.5 6.8 %all-to-all-start.9 = ((f32[8,1,1536]{2,1,0:T(1,128)}), f32[8,1,1536]{2,1,0:T(1,128)S(1)}, u32[]{:S(2)}, u32[]{:S(2)}) async-start(f32[8,1,1536]{2,1,0:T(1,128)} %reshape.500), calls=%async_computation.9 | async-start | bytes 98304 | tf_op jit(solution)/shard_map/all_to_all | solution.py:203
  323.1 3.0 reshape.497
  326.2 4.3 copy.190
  330.4 4.0 reduce.14
  335.7 6.2 %all-to-all-start.8 = ((f32[32,1,384]{2,1,0:T(1,128)}), f32[32,1,384]{2,1,0:T(1,128)S(1)}, u32[]{:S(2)}, u32[]{:S(2)}) async-start(f32[32,1,384]{2,1,0:T(1,128)} %reshape.498), calls=%async_computation.8 | async-start | bytes 98304 | tf_op jit(solution)/shard_map/all_to_all | solution.py:212
  342.8 79.2 %all-reduce = (f32[3,64,64]{2,1,0:T(8,128)S(1)}, f32[64,3]{0,1:T(4,128)S(1)}) all-reduce(f32[3,64,64]{2,1,0:T(8,128)S(1)} %pad_maximum_fusion.6, f32[64,3]{0,1:T(4,128)S(1)} %fusion.359), channel_id=1, replica_groups=mesh['rows'=8,'cols'=32] {'rows','cols'}, use_global_device_ids=true, to_apply=%region_2.0 | all-reduce | flops 12480 | bytes 99840 | tf_op jit(solution)/shard_map/psum | solution.py:302
  422.8 3.0 reshape.501
  425.8 4.0 copy.195
  429.8 3.2 reduce.18
  434.2 4.7 all-to-all-start.10
  443.6 2.7 all-to-all-done.10
  451.9 4.8 all-to-all-start.12
  458.4 5.6 %all-to-all-done.12 = f32[32,1,384]{2,1,0:T(1,128)S(1)} async-done(((f32[32,1,384]{2,1,0:T(1,128)}), f32[32,1,384]{2,1,0:T(1,128)S(1)}, u32[]{:S(2)}, u32[]{:S(2)}) %all-to-all-start.12) | async-done | bytes 49184 | tf_op jit(solution)/shard_map/all_to_all | solution.py:233
  464.0 3.9 all-to-all-start.11
  469.7 5.6 %all-to-all-done.11 = f32[32,1,384]{2,1,0:T(1,128)S(1)} async-done(((f32[32,1,384]{2,1,0:T(1,128)}), f32[32,1,384]{2,1,0:T(1,128)S(1)}, u32[]{:S(2)}, u32[]{:S(2)}) %all-to-all-start.11) | async-done | bytes 49184 | tf_op jit(solution)/shard_map/all_to_all | solution.py:232
  477.7 5.1 all-to-all-start.13
  482.8 63.4 %all-reduce.4.cloned.1.call-done = (f32[3,128,64]{1,2,0:T(8,128)}, f32[3,128,64]{1,2,0:T(8,128)}) async-done(((f32[3,128,64]{1,2,0:T(8,128)}, f32[3,128,64]{1,2,0:T(8,128)}), (f32[3,128,64]{1,2,0:T(8,128)}, f32[3,128,64]{1,2,0:T(8,128)})) %all-reduce.4.cloned.1.call-update) | async-done | bytes 196624 | tf_op jit(solution)/shard_map/psum | solution.py:302
  546.2 1.6 broadcast_multiply_fusion.1
  (251 shorter events, 82.8 us)
Async XLA Ops:
  8.0 24.8 %copy-start.38 = (f32[64]{0:T(128)}, f32[64]{0:T(128)S(1)}, u32[]{:S(2)}) copy-start(f32[64]{0:T(128)S(1)} %get-tuple-element.29) | copy-start | bytes 772
  8.0 24.8 %copy-start.40 = (f32[64]{0:T(128)}, f32[64]{0:T(128)S(1)}, u32[]{:S(2)}) copy-start(f32[64]{0:T(128)S(1)} %get-tuple-element.30) | copy-start | bytes 772
  9.2 37.5 %copy-start.5 = (bf16[64,4096]{1,0:T(8,128)(2,1)}, bf16[64,4096]{1,0:T(8,128)(2,1)S(1)}, u32[]{:S(2)}) copy-start(bf16[64,4096]{1,0:T(8,128)(2,1)S(1)} %fusion.33) | copy-start | bytes 1572868
  9.2 23.6 %copy-start.24 = (bf16[3,128,64]{1,2,0:T(8,128)(2,1)S(1)}, bf16[3,128,64]{1,2,0:T(8,128)(2,1)}, u32[]{:S(2)}) copy-start(bf16[3,128,64]{1,2,0:T(8,128)(2,1)} %param.12) | copy-start | bytes 147460
  9.3 37.5 %collective-permute-start = (bf16[64,256]{1,0:T(8,128)(2,1)S(1)}, bf16[64,256]{1,0:T(8,128)(2,1)S(1)}, u32[]{:S(2)}, u32[]{:S(2)}) collective-permute-start(bf16[64,256]{1,0:T(8,128)(2,1)S(1)} %slice.140), channel_id=1, source_target_pairs={{0,1},{1,2},{2,3},{3,4},{4,5},{5,6},{6,7},{7,8},{8,9},{9,10},{10,1... | collective-permute-start | bytes 98312 | tf_op jit(solution)/shard_map/ppermute | solution.py:13
  32.1 1.3 copy-start.45
  32.1 14.7 %copy-start.23 = (bf16[3,128,64]{1,2,0:T(8,128)(2,1)S(1)}, bf16[3,128,64]{1,2,0:T(8,128)(2,1)}, u32[]{:S(2)}) copy-start(bf16[3,128,64]{1,2,0:T(8,128)(2,1)} %param.13) | copy-start | bytes 147460
  34.3 13.0 %copy-start.18 = (f32[2,64,64]{2,1,0:T(8,128)}, f32[2,64,64]{2,1,0:T(8,128)S(1)}, u32[]{:S(2)}) copy-start(f32[2,64,64]{2,1,0:T(8,128)S(1)} %select_bitcast_fusion) | copy-start | bytes 98308
  47.4 0.8 copy-start.39
  47.4 0.8 copy-start.41
  48.2 2.8 copy-start.2
  48.5 29.5 %copy-start = (bf16[64,4096]{1,0:T(8,128)(2,1)}, bf16[64,4096]{1,0:T(8,128)(2,1)S(1)}, u32[]{:S(2)}) copy-start(bf16[64,4096]{1,0:T(8,128)(2,1)S(1)} %get-tuple-element.34) | copy-start | bytes 1572868
  48.6 3.1 collective-permute-start.1
  52.7 4.9 copy-start.4
  53.0 5.1 collective-permute-start.2
  57.6 1.1 copy-start.20
  60.9 6.2 %collective-permute-start.3 = (f32[64,256]{1,0:T(8,128)S(1)}, f32[64,256]{1,0:T(8,128)S(1)}, u32[]{:S(2)}, u32[]{:S(2)}) collective-permute-start(f32[64,256]{1,0:T(8,128)S(1)} %slice.149), channel_id=1, source_target_pairs={{1,0},{2,1},{3,2},{4,3},{5,4},{6,5},{7,6},{8,7},{9,8},{10,9},{11,1... | collective-permute-start | bytes 196616 | tf_op jit(solution)/shard_map/ppermute | solution.py:13
  68.5 9.6 %copy-start.12 = (bf16[64,4096]{1,0:T(8,128)(2,1)}, bf16[64,4096]{1,0:T(8,128)(2,1)S(1)}, u32[]{:S(2)}) copy-start(bf16[64,4096]{1,0:T(8,128)(2,1)S(1)} %get-tuple-element.11) | copy-start | bytes 1572868
  68.5 9.6 %copy-start.13 = (bf16[64,4096]{1,0:T(8,128)(2,1)}, bf16[64,4096]{1,0:T(8,128)(2,1)S(1)}, u32[]{:S(2)}) copy-start(bf16[64,4096]{1,0:T(8,128)(2,1)S(1)} %get-tuple-element.12) | copy-start | bytes 1572868
  68.8 5.6 %collective-permute-start.4 = (f32[64,256]{1,0:T(8,128)S(1)}, f32[64,256]{1,0:T(8,128)S(1)}, u32[]{:S(2)}, u32[]{:S(2)}) collective-permute-start(f32[64,256]{1,0:T(8,128)S(1)} %slice.150), channel_id=1, source_target_pairs={{1,0},{2,1},{3,2},{4,3},{5,4},{6,5},{7,6},{8,7},{9,8},{10,9},{11,1... | collective-permute-start | bytes 196616 | tf_op jit(solution)/shard_map/ppermute | solution.py:13
  75.8 5.9 %copy-start.7 = (bf16[64,4096]{1,0:T(8,128)(2,1)}, bf16[64,4096]{1,0:T(8,128)(2,1)S(1)}, u32[]{:S(2)}) copy-start(bf16[64,4096]{1,0:T(8,128)(2,1)S(1)} %get-tuple-element.9) | copy-start | bytes 1572868
  75.8 5.9 %copy-start.10 = (bf16[64,4096]{1,0:T(8,128)(2,1)}, bf16[64,4096]{1,0:T(8,128)(2,1)S(1)}, u32[]{:S(2)}) copy-start(bf16[64,4096]{1,0:T(8,128)(2,1)S(1)} %get-tuple-element.10) | copy-start | bytes 1572868
  76.1 5.6 %collective-permute-start.5 = (f32[64,256]{1,0:T(8,128)S(1)}, f32[64,256]{1,0:T(8,128)S(1)}, u32[]{:S(2)}, u32[]{:S(2)}) collective-permute-start(f32[64,256]{1,0:T(8,128)S(1)} %slice.151), channel_id=1, source_target_pairs={{1,0},{2,1},{3,2},{4,3},{5,4},{6,5},{7,6},{8,7},{9,8},{10,9},{11,1... | collective-permute-start | bytes 196616 | tf_op jit(solution)/shard_map/ppermute | solution.py:13
  79.2 3.2 copy-start.42
  111.4 28.1 %all-to-all-start = ((f32[8,1,1536]{2,1,0:T(1,128)}), f32[8,1,1536]{2,1,0:T(1,128)S(1)}, u32[]{:S(2)}, u32[]{:S(2)}) async-start(f32[8,1,1536]{2,1,0:T(1,128)} %reshape.486), calls=%async_computation | async-start | bytes 98304 | tf_op jit(solution)/shard_map/all_to_all | solution.py:138
  140.2 6.9 %copy-start.43 = (f32[8]{0:T(128)S(1)}, f32[8]{0:T(128)}, u32[]{:S(2)}) copy-start(f32[8]{0:T(128)} %get-tuple-element.38) | copy-start | bytes 100
  140.3 6.9 %copy-start.44 = (f32[8]{0:T(128)S(1)}, f32[8]{0:T(128)}, u32[]{:S(2)}) copy-start(f32[8]{0:T(128)} %get-tuple-element.39) | copy-start | bytes 100
  146.9 24.3 %copy-start.1 = (bf16[64,4096]{1,0:T(8,128)(2,1)S(1)}, bf16[64,4096]{1,0:T(8,128)(2,1)}, u32[]{:S(2)}) copy-start(bf16[64,4096]{1,0:T(8,128)(2,1)} %copy-done) | copy-start | bytes 1572868
  154.2 19.4 %copy-start.25 = (f32[3,8,1,512]{3,1,0,2:T(8,128)S(1)}, f32[3,8,1,512]{3,1,0,2:T(8,128)}, u32[]{:S(2)}) copy-start(f32[3,8,1,512]{3,1,0,2:T(8,128)} %get-tuple-element.21) | copy-start | bytes 147460
  156.7 23.8 %all-to-all-start.1 = ((f32[32,1,384]{2,1,0:T(1,128)}), f32[32,1,384]{2,1,0:T(1,128)S(1)}, u32[]{:S(2)}, u32[]{:S(2)}) async-start(f32[32,1,384]{2,1,0:T(1,128)} %reshape.488), calls=%async_computation.1 | async-start | bytes 98304 | tf_op jit(solution)/shard_map/all_to_all | solution.py:146
  180.5 15.1 %all-to-all-start.2 = ((f32[32,1,384]{2,1,0:T(1,128)}), f32[32,1,384]{2,1,0:T(1,128)S(1)}, u32[]{:S(2)}, u32[]{:S(2)}) async-start(f32[32,1,384]{2,1,0:T(1,128)} %reshape.490), calls=%async_computation.2 | async-start | bytes 98304 | tf_op jit(solution)/shard_map/all_to_all | solution.py:153
  197.6 15.1 %copy-start.8 = (bf16[64,4096]{1,0:T(8,128)(2,1)S(1)}, bf16[64,4096]{1,0:T(8,128)(2,1)}, u32[]{:S(2)}) copy-start(bf16[64,4096]{1,0:T(8,128)(2,1)} %copy-done.7) | copy-start | bytes 1572868
  206.4 13.6 %all-to-all-start.3 = ((f32[32,1,384]{2,1,0:T(1,128)}), f32[32,1,384]{2,1,0:T(1,128)}, u32[]{:S(2)}, u32[]{:S(2)}) async-start(f32[32,1,384]{2,1,0:T(1,128)} %reshape.492), calls=%async_computation.3 | async-start | bytes 98304 | tf_op jit(solution)/shard_map/all_to_all | solution.py:170
  212.7 11.9 %copy-start.3 = (bf16[64,4096]{1,0:T(8,128)(2,1)S(1)}, bf16[64,4096]{1,0:T(8,128)(2,1)}, u32[]{:S(2)}) copy-start(bf16[64,4096]{1,0:T(8,128)(2,1)} %copy-done.2) | copy-start | bytes 1572868
  215.1 21.7 %copy-start.6 = (bf16[64,4096]{1,0:T(8,128)(2,1)S(1)}, bf16[64,4096]{1,0:T(8,128)(2,1)}, u32[]{:S(2)}) copy-start(bf16[64,4096]{1,0:T(8,128)(2,1)} %copy-done.5) | copy-start | bytes 1572868
  220.0 12.0 %all-to-all-start.5 = ((f32[32,1,384]{2,1,0:T(1,128)}), f32[32,1,384]{2,1,0:T(1,128)}, u32[]{:S(2)}, u32[]{:S(2)}) async-start(f32[32,1,384]{2,1,0:T(1,128)} %reshape.494), calls=%async_computation.5 | async-start | bytes 98304 | tf_op jit(solution)/shard_map/all_to_all | solution.py:171
  225.4 11.3 %copy-start.9 = (bf16[64,4096]{1,0:T(8,128)(2,1)S(1)}, bf16[64,4096]{1,0:T(8,128)(2,1)}, u32[]{:S(2)}) copy-start(bf16[64,4096]{1,0:T(8,128)(2,1)} %copy-done.7) | copy-start | bytes 1572868
  225.4 11.3 %copy-start.11 = (bf16[64,4096]{1,0:T(8,128)(2,1)S(1)}, bf16[64,4096]{1,0:T(8,128)(2,1)}, u32[]{:S(2)}) copy-start(bf16[64,4096]{1,0:T(8,128)(2,1)} %copy-done.10) | copy-start | bytes 1572868
  225.4 11.3 %copy-start.30 = (bf16[64,256]{1,0:T(8,128)(2,1)S(1)}, bf16[64,256]{1,0:T(8,128)(2,1)}, u32[]{:S(2)}) copy-start(bf16[64,256]{1,0:T(8,128)(2,1)} %copy-done.29) | copy-start | bytes 98308
  232.0 10.4 %all-to-all-start.4 = ((f32[3,8,512]{2,0,1:T(4,128)}), f32[3,8,512]{2,0,1:T(4,128)S(1)}, u32[]{:S(2)}, u32[]{:S(2)}) async-start(f32[3,8,512]{2,0,1:T(4,128)} %reshape.475), calls=%async_computation.4 | async-start | bytes 131072 | tf_op jit(solution)/shard_map/all_to_all | solution.py:174
  237.3 17.6 %copy-start.16 = (f32[64,64]{0,1:T(8,128)S(1)}, f32[64,64]{0,1:T(8,128)}, u32[]{:S(2)}) copy-start(f32[64,64]{0,1:T(8,128)} %copy.171) | copy-start | bytes 49156
  237.3 17.6 %copy-start.17 = (f32[64,64]{0,1:T(8,128)S(1)}, f32[64,64]{0,1:T(8,128)}, u32[]{:S(2)}) copy-start(f32[64,64]{0,1:T(8,128)} %copy.174) | copy-start | bytes 49156
  237.4 18.4 %copy-start.19 = (f32[2,64,64]{2,1,0:T(8,128)S(1)}, f32[2,64,64]{2,1,0:T(8,128)}, u32[]{:S(2)}) copy-start(f32[2,64,64]{2,1,0:T(8,128)} %copy-done.18) | copy-start | bytes 98308
  237.4 18.4 %copy-start.21 = (f32[1,64,64]{2,1,0:T(8,128)S(1)}, f32[1,64,64]{2,1,0:T(8,128)}, u32[]{:S(2)}) copy-start(f32[1,64,64]{2,1,0:T(8,128)} %slice.152) | copy-start | bytes 49156
  242.4 11.7 %all-to-all-start.6 = ((f32[3,8,512]{2,0,1:T(4,128)}), f32[3,8,512]{2,0,1:T(4,128)S(1)}, u32[]{:S(2)}, u32[]{:S(2)}) async-start(f32[3,8,512]{2,0,1:T(4,128)} %reshape.476), calls=%async_computation.6 | async-start | bytes 131072 | tf_op jit(solution)/shard_map/all_to_all | solution.py:181
  246.9 11.1 %copy-start.14 = (f32[64,64]{1,0:T(8,128)S(1)}, f32[64,64]{1,0:T(8,128)}, u32[]{:S(2)}) copy-start(f32[64,64]{1,0:T(8,128)} %get-tuple-element.40) | copy-start | bytes 49156
  246.9 11.1 %copy-start.15 = (f32[64,64]{1,0:T(8,128)S(1)}, f32[64,64]{1,0:T(8,128)}, u32[]{:S(2)}) copy-start(f32[64,64]{1,0:T(8,128)} %get-tuple-element.41) | copy-start | bytes 49156
  255.7 4.3 copy-start.28
  281.9 7.3 %copy-start.33 = (f32[1,128,64]{1,2,0:T(8,128)S(1)}, f32[1,128,64]{1,2,0:T(8,128)}, u32[]{:S(2)}) copy-start(f32[1,128,64]{1,2,0:T(8,128)} %convolution_bitcast_fusion.11) | copy-start | bytes 98308
  281.9 7.4 %copy-start.34 = (f32[1,128,64]{1,2,0:T(8,128)S(1)}, f32[1,128,64]{1,2,0:T(8,128)}, u32[]{:S(2)}) copy-start(f32[1,128,64]{1,2,0:T(8,128)} %convolution_bitcast_fusion.12) | copy-start | bytes 98308
  285.6 29.9 %all-to-all-start.7 = ((f32[8,1,1536]{2,1,0:T(1,128)}), f32[8,1,1536]{2,1,0:T(1,128)S(1)}, u32[]{:S(2)}, u32[]{:S(2)}) async-start(f32[8,1,1536]{2,1,0:T(1,128)} %reshape.496), calls=%async_computation.7 | async-start | bytes 98304 | tf_op jit(solution)/shard_map/all_to_all | solution.py:196
  289.0 257.3 %all-reduce.4.cloned.1.call-start = ((), (), s32[]{:S(2)}) async-start(), calls=%async_computation.14 | async-start | bytes 393216 | tf_op jit(solution)/shard_map/psum | solution.py:302
  311.8 10.6 %copy-start.26 = (f32[1,64,64]{2,1,0:T(8,128)S(1)}, f32[1,64,64]{2,1,0:T(8,128)}, u32[]{:S(2)}) copy-start(f32[1,64,64]{2,1,0:T(8,128)} %convolution_bitcast_fusion.18) | copy-start | bytes 49156
  311.8 10.6 %copy-start.27 = (f32[1,64,64]{2,1,0:T(8,128)S(1)}, f32[1,64,64]{2,1,0:T(8,128)}, u32[]{:S(2)}) copy-start(f32[1,64,64]{2,1,0:T(8,128)} %convolution_bitcast_fusion.19) | copy-start | bytes 49156
  311.8 10.6 %copy-start.32 = (f32[1,64,64]{2,1,0:T(8,128)S(1)}, f32[1,64,64]{2,1,0:T(8,128)}, u32[]{:S(2)}) copy-start(f32[1,64,64]{2,1,0:T(8,128)} %convolution_bitcast_fusion.17) | copy-start | bytes 49156
  315.5 20.2 %all-to-all-start.9 = ((f32[8,1,1536]{2,1,0:T(1,128)}), f32[8,1,1536]{2,1,0:T(1,128)S(1)}, u32[]{:S(2)}, u32[]{:S(2)}) async-start(f32[8,1,1536]{2,1,0:T(1,128)} %reshape.500), calls=%async_computation.9 | async-start | bytes 98304 | tf_op jit(solution)/shard_map/all_to_all | solution.py:203
  330.4 11.5 %copy-start.22 = (f32[3,4096]{1,0:T(4,128)S(1)}, f32[3,4096]{1,0:T(4,128)}, u32[]{:S(2)}) copy-start(f32[3,4096]{1,0:T(4,128)} %param.9) | copy-start | bytes 147460
  335.7 98.6 %all-to-all-start.8 = ((f32[32,1,384]{2,1,0:T(1,128)}), f32[32,1,384]{2,1,0:T(1,128)S(1)}, u32[]{:S(2)}, u32[]{:S(2)}) async-start(f32[32,1,384]{2,1,0:T(1,128)} %reshape.498), calls=%async_computation.8 | async-start | bytes 98304 | tf_op jit(solution)/shard_map/all_to_all | solution.py:212
  434.2 12.0 %all-to-all-start.10 = ((f32[32,1,384]{2,1,0:T(1,128)}), f32[32,1,384]{2,1,0:T(1,128)S(1)}, u32[]{:S(2)}, u32[]{:S(2)}) async-start(f32[32,1,384]{2,1,0:T(1,128)} %reshape.502), calls=%async_computation.10 | async-start | bytes 98304 | tf_op jit(solution)/shard_map/all_to_all | solution.py:219
  442.0 8.1 %copy-start.36 = (f32[8,32]{1,0:T(8,128)S(1)}, f32[8,32]{1,0:T(8,128)}, u32[]{:S(2)}) copy-start(f32[8,32]{1,0:T(8,128)} %get-tuple-element.36) | copy-start | bytes 3076
  442.0 8.1 %copy-start.37 = (f32[8,32]{1,0:T(8,128)S(1)}, f32[8,32]{1,0:T(8,128)}, u32[]{:S(2)}) copy-start(f32[8,32]{1,0:T(8,128)} %get-tuple-element.37) | copy-start | bytes 3076
  451.9 12.1 %all-to-all-start.12 = ((f32[32,1,384]{2,1,0:T(1,128)}), f32[32,1,384]{2,1,0:T(1,128)S(1)}, u32[]{:S(2)}, u32[]{:S(2)}) async-start(f32[32,1,384]{2,1,0:T(1,128)} %reshape.506), calls=%async_computation.12 | async-start | bytes 98304 | tf_op jit(solution)/shard_map/all_to_all | solution.py:233
  464.0 11.3 %all-to-all-start.11 = ((f32[32,1,384]{2,1,0:T(1,128)}), f32[32,1,384]{2,1,0:T(1,128)S(1)}, u32[]{:S(2)}, u32[]{:S(2)}) async-start(f32[32,1,384]{2,1,0:T(1,128)} %reshape.504), calls=%async_computation.11 | async-start | bytes 98304 | tf_op jit(solution)/shard_map/all_to_all | solution.py:232
  477.7 70.2 %all-to-all-start.13 = ((f32[3,8,512]{2,0,1:T(4,128)}), f32[3,8,512]{2,0,1:T(4,128)S(1)}, u32[]{:S(2)}, u32[]{:S(2)}) async-start(f32[3,8,512]{2,0,1:T(4,128)} %copy.204), calls=%async_computation.13 | async-start | bytes 131072 | tf_op jit(solution)/shard_map/all_to_all | solution.py:241
  (3 other events, 2.0 us)
Sparse Core Ops, SparseCore 0:
  296.0 250.2 all-reduce.3
where the time goes:
time: 566 us; the launch traced here: 556 us
  starting transfers between devices  114 us (20%)
  waiting for transfers between devices  109 us (19%)
  other arithmetic  97.2 us (17%)
  local copies, waits for them, and re-layouts  90 us (16%)
  blocking collectives  79.2 us (14%)
  matrix products  40.8 us (7%)
  between operations  25.4 us (4%)
    psum x1, blocking collectives, local(): lax.psum((jnp.stack(grads_now), jnp.stack(grads_past), jnp.stack(grads_mi...  79.2 us
    unnamed x8, other arithmetic  76 us
    psum x1, waiting for transfers between devices, local(): lax.psum((jnp.stack(grads_now), jnp.stack(grads_past), jnp.stack(grads_mi...  63.4 us
    unnamed x117, local copies, waits for them, and re-layouts  39.2 us
    all_to_all x1, starting transfers between devices, per_axis_filter(): lax.all_to_all(signal.reshape(3, 1, segment), 'rows', split_axis=2, conca...  21 us
    ppermute x6, starting transfers between devices, from_behind(): return lax.ppermute(array, axis, pairs)  16.5 us
    all_to_all x1, starting transfers between devices, per_axis_filter(): lax.all_to_all(signals[0].reshape(signal_count, rows_count, 1, piece_len)...  14.5 us
    gather x2, local copies, waits for them, and re-layouts, local_section(): weights = jnp.take(psd_weight, bins_here, axis=1)  11.5 us
  transfers between devices with their start and end apart: 21, of which 15 were waited for; matrix products, arithmetic and copies ran while one was open for 23% of the time, Pallas kernels for 0%

commit v1 on v0

--- a/solution.py
+++ b/solution.py
@@ -300,8 +300,10 @@
     input_grad = jnp.dot(lift_weight.T, grad_field, precision=lax.Precision.HIGHEST)
     lift_part = jnp.dot(grad_field, whitened.T, precision=lax.Precision.HIGHEST)
     summed = lax.psum(
-        (jnp.stack(grads_now), jnp.stack(grads_past), jnp.stack(grads_mix), lift_part),
-        ("rows", "cols"),
+        lax.psum(
+            (jnp.stack(grads_now), jnp.stack(grads_past), jnp.stack(grads_mix), lift_part), "cols"
+        ),
+        "rows",
     )
     scaling = 1.0 / math.sqrt(float(segment * lax.axis_size("rows") * lax.axis_size("cols")))
     data_grad = per_axis_filter(input_grad, psd_bin, psd_weight)

time: 566 us -> 634 us (1.12)
  the two profiles are of different devices: /device:TPU:1 before, /device:TPU:2 now
where the time goes in v1:
time: 634 us; the launch traced here: 624 us
  blocking collectives  152 us (24%)
  starting transfers between devices  121 us (19%)
  waiting for transfers between devices  106 us (17%)
  other arithmetic  95.4 us (15%)
  local copies, waits for them, and re-layouts  86.5 us (14%)
  matrix products  37.7 us (6%)
  between operations  25.2 us (4%)
    psum x1, blocking collectives, local(): lax.psum((jnp.stack(grads_now), jnp.stack(grads_past), jnp.stack(grads_mi...  120 us
    unnamed x8, other arithmetic  74.8 us
    psum x1, waiting for transfers between devices, local(): lax.psum(lax.psum((jnp.stack(grads_now), jnp.stack(grads_past), jnp.stack...  61.7 us
    unnamed x101, local copies, waits for them, and re-layouts  39.1 us
    psum x1, blocking collectives, local(): lax.psum(lax.psum((jnp.stack(grads_now), jnp.stack(grads_past), jnp.stack...  32 us
    all_to_all x1, starting transfers between devices, per_axis_filter(): lax.all_to_all(signals[0].reshape(signal_count, rows_count, 1, piece_len)...  18.4 us
    all_to_all x1, starting transfers between devices, per_axis_filter(): lax.all_to_all(signal.reshape(3, 1, segment), 'rows', split_axis=2, conca...  17.7 us
    ppermute x6, starting transfers between devices, from_behind(): return lax.ppermute(array, axis, pairs)  16.8 us
  transfers between devices with their start and end apart: 22, of which 15 were waited for; matrix products, arithmetic and copies ran while one was open for 24% of the time, Pallas kernels for 0%

profile of v1, /device:TPU:2, one launch (start us, length us, event | category | flops | bytes accessed | tf_op | source)
XLA Modules:
  0.0 624.0 jit_solution(14151084490687440475)
XLA Ops:
  9.9 1.9 collective-permute-start
  13.0 1.4 reduce.3
  16.1 1.4 fusion.349
  19.9 10.8 %gather_fusion = f32[4096,2]{1,0:T(8,128)S(1)} fusion(f32[2,1024]{0,1:T(8,128)S(1)} %copy.178, s32[4096]{0:T(1024)S(1)} %broadcast_clamp_fusion), kind=kCustom, calls=%fused_computation | custom fusion | bytes 81920 | tf_op jit(solution)/shard_map/jit(_take)/gather | solution.py:110
  44.0 1.3 fusion.2
  46.5 3.5 collective-permute-start.1
  53.0 1.9 collective-permute-start.2
  55.4 2.8 collective-permute-done.2
  58.8 1.3 convolution_bitcast_fusion.17
  62.2 1.9 collective-permute-start.3
  68.8 3.9 collective-permute-start.4
  76.1 3.7 collective-permute-start.5
  83.1 3.7 copy.151
  87.3 20.4 %reduce.4 = f32[4096,3]{1,0:T(8,128)} reduce(f32[4096,1,3]{2,1,0:T(1,128)} %bitcast.335, f32[]{:T(128)} %broadcast.734), dimensions={1}, to_apply=%bitcast.265.reduce_sub_computation | reduce | bytes 98308
  107.8 3.7 reshape.486
  111.5 17.7 %all-to-all-start = ((f32[8,1,1536]{2,1,0:T(1,128)}), f32[8,1,1536]{2,1,0:T(1,128)S(1)}, u32[]{:S(2)}, u32[]{:S(2)}) async-start(f32[8,1,1536]{2,1,0:T(1,128)} %reshape.486), calls=%async_computation | async-start | bytes 98304 | tf_op jit(solution)/shard_map/all_to_all | solution.py:138
  129.2 2.2 convolution_bitcast_fusion.16
  131.4 6.0 all-to-all-done
  138.2 4.4 reshape.487
  142.6 2.2 copy.231
  145.9 2.0 copy.153
  147.9 4.3 reduce.6
  152.1 2.5 reshape.488
  154.6 18.4 %all-to-all-start.1 = ((f32[32,1,384]{2,1,0:T(1,128)}), f32[32,1,384]{2,1,0:T(1,128)S(1)}, u32[]{:S(2)}, u32[]{:S(2)}) async-start(f32[32,1,384]{2,1,0:T(1,128)} %reshape.488), calls=%async_computation.1 | async-start | bytes 98304 | tf_op jit(solution)/shard_map/all_to_all | solution.py:146
  174.7 3.3 reduce.8
  179.3 7.9 %all-to-all-start.2 = ((f32[32,1,384]{2,1,0:T(1,128)}), f32[32,1,384]{2,1,0:T(1,128)S(1)}, u32[]{:S(2)}, u32[]{:S(2)}) async-start(f32[32,1,384]{2,1,0:T(1,128)} %reshape.490), calls=%async_computation.2 | async-start | bytes 98304 | tf_op jit(solution)/shard_map/all_to_all | solution.py:153
  191.8 1.5 all-to-all-done.2
  197.2 2.3 multiply_add_fusion.1
  201.5 5.9 all-to-all-start.3
  207.4 1.4 pad_maximum_fusion.4
  209.9 3.8 all-to-all-done.3
  213.7 4.9 all-to-all-start.5
  218.7 1.3 convolution_bitcast_fusion.13
  221.9 3.1 all-to-all-done.5
  225.0 3.4 all-to-all-start.4
  231.1 5.6 all-to-all-done.4
  236.6 3.5 all-to-all-start.6
  241.0 7.4 %all-to-all-done.6 = f32[3,8,512]{2,0,1:T(4,128)S(1)} async-done(((f32[3,8,512]{2,0,1:T(4,128)}), f32[3,8,512]{2,0,1:T(4,128)S(1)}, u32[]{:S(2)}, u32[]{:S(2)}) %all-to-all-start.6) | async-done | bytes 49184 | tf_op jit(solution)/shard_map/all_to_all | solution.py:181
  254.4 2.4 copy.188
  256.9 19.4 %reduce.12 = f32[4096,3]{1,0:T(8,128)} reduce(f32[4096,1,3]{2,1,0:T(1,128)S(1)} %bitcast.337, f32[]{:T(128)} %broadcast.734), dimensions={1}, to_apply=%bitcast.275.reduce_sub_computation | reduce | bytes 98308
  276.3 3.7 reshape.496
  280.1 3.6 all-to-all-start.7
  283.7 2.4 copy.193
  286.1 19.4 %reduce.16 = f32[4096,3]{1,0:T(8,128)} reduce(f32[4096,1,3]{2,1,0:T(1,128)S(1)} %bitcast.338, f32[]{:T(128)} %broadcast.734), dimensions={1}, to_apply=%bitcast.279.reduce_sub_computation | reduce | bytes 98308
  305.5 3.7 reshape.500
  309.3 7.2 %all-to-all-start.9 = ((f32[8,1,1536]{2,1,0:T(1,128)}), f32[8,1,1536]{2,1,0:T(1,128)S(1)}, u32[]{:S(2)}, u32[]{:S(2)}) async-start(f32[8,1,1536]{2,1,0:T(1,128)} %reshape.500), calls=%async_computation.9 | async-start | bytes 98304 | tf_op jit(solution)/shard_map/all_to_all | solution.py:203
  317.4 120.0 %all-reduce = (f32[3,64,64]{2,1,0:T(8,128)S(1)}, f32[64,3]{0,1:T(4,128)S(1)}) all-reduce(f32[3,64,64]{2,1,0:T(8,128)S(1)} %pad_maximum_fusion.6, f32[64,3]{0,1:T(4,128)S(1)} %fusion.359), channel_id=1, replica_groups=mesh['rows'=8,'cols'=32] {'cols'}, use_global_device_ids=true, to_apply=%region_4.0 | all-reduce | flops 12480 | bytes 99840 | tf_op jit(solution)/shard_map/psum | solution.py:303
  438.2 3.0 reshape.497
  441.2 4.0 copy.190
  445.2 3.3 reduce.14
  449.7 9.1 %all-to-all-start.8 = ((f32[32,1,384]{2,1,0:T(1,128)}), f32[32,1,384]{2,1,0:T(1,128)S(1)}, u32[]{:S(2)}, u32[]{:S(2)}) async-start(f32[32,1,384]{2,1,0:T(1,128)} %reshape.498), calls=%async_computation.8 | async-start | bytes 98304 | tf_op jit(solution)/shard_map/all_to_all | solution.py:212
  458.8 32.0 %all-reduce.2 = (f32[3,64,64]{2,1,0:T(8,128)S(1)}, f32[64,3]{0,1:T(4,128)S(1)}) all-reduce(f32[3,64,64]{2,1,0:T(8,128)S(1)} %get-tuple-element.5, f32[64,3]{0,1:T(4,128)S(1)} %get-tuple-element.6), channel_id=1, replica_groups=mesh['rows'=8,'cols'=32] {'rows'}, use_global_device_ids=true, to_apply=%region_5.0 | all-reduce | flops 12480 | bytes 99840 | tf_op jit(solution)/shard_map/psum | solution.py:302
  491.7 3.0 reshape.501
  494.7 4.0 copy.195
  498.7 3.3 reduce.18
  503.2 7.8 %all-to-all-start.10 = ((f32[32,1,384]{2,1,0:T(1,128)}), f32[32,1,384]{2,1,0:T(1,128)S(1)}, u32[]{:S(2)}, u32[]{:S(2)}) async-start(f32[32,1,384]{2,1,0:T(1,128)} %reshape.502), calls=%async_computation.10 | async-start | bytes 98304 | tf_op jit(solution)/shard_map/all_to_all | solution.py:219
  515.7 1.5 all-to-all-done.10
  522.8 5.9 all-to-all-start.12
  530.4 4.6 all-to-all-done.12
  535.0 4.9 all-to-all-start.11
  542.0 4.3 all-to-all-done.11
  548.7 4.4 all-to-all-start.13
  553.1 61.7 %all-reduce.9.cloned.1.call-done = (f32[3,128,64]{1,2,0:T(8,128)}, f32[3,128,64]{1,2,0:T(8,128)}) async-done(((f32[3,128,64]{1,2,0:T(8,128)}, f32[3,128,64]{1,2,0:T(8,128)}), (f32[3,128,64]{1,2,0:T(8,128)}, f32[3,128,64]{1,2,0:T(8,128)})) %all-reduce.9.cloned.1.call-update) | async-done | bytes 196624 | tf_op jit(solution)/shard_map/psum | solution.py:302
  614.7 1.6 broadcast_multiply_fusion.1
  (239 shorter events, 80.1 us)
Async XLA Ops:
  8.0 10.3 %copy-start.25 = (f32[64]{0:T(128)}, f32[64]{0:T(128)S(1)}, u32[]{:S(2)}) copy-start(f32[64]{0:T(128)S(1)} %get-tuple-element.32) | copy-start | bytes 772
  8.0 10.3 %copy-start.28 = (f32[64]{0:T(128)}, f32[64]{0:T(128)S(1)}, u32[]{:S(2)}) copy-start(f32[64]{0:T(128)S(1)} %get-tuple-element.33) | copy-start | bytes 772
  8.0 10.3 %copy-start.31 = (f32[64]{0:T(128)}, f32[64]{0:T(128)S(1)}, u32[]{:S(2)}) copy-start(f32[64]{0:T(128)S(1)} %get-tuple-element.34) | copy-start | bytes 772
  9.2 34.7 %copy-start = (bf16[64,4096]{1,0:T(8,128)(2,1)}, bf16[64,4096]{1,0:T(8,128)(2,1)S(1)}, u32[]{:S(2)}) copy-start(bf16[64,4096]{1,0:T(8,128)(2,1)S(1)} %fusion.33) | copy-start | bytes 1572868
  9.3 22.1 %copy-start.12 = (bf16[3,128,64]{1,2,0:T(8,128)(2,1)S(1)}, bf16[3,128,64]{1,2,0:T(8,128)(2,1)}, u32[]{:S(2)}) copy-start(bf16[3,128,64]{1,2,0:T(8,128)(2,1)} %param.12) | copy-start | bytes 147460
  9.9 34.1 %collective-permute-start = (bf16[64,256]{1,0:T(8,128)(2,1)}, bf16[64,256]{1,0:T(8,128)(2,1)}, u32[]{:S(2)}, u32[]{:S(2)}) collective-permute-start(bf16[64,256]{1,0:T(8,128)(2,1)} %slice.140), channel_id=1, source_target_pairs={{0,1},{1,2},{2,3},{3,4},{4,5},{5,6},{6,7},{7,8},{8,9},{9,10},{10,1... | collective-permute-start | bytes 98312 | tf_op jit(solution)/shard_map/ppermute | solution.py:13
  18.9 12.4 %copy-start.26 = (f32[64]{0:T(128)S(1)}, f32[64]{0:T(128)}, u32[]{:S(2)}) copy-start(f32[64]{0:T(128)} %copy-done.25) | copy-start | bytes 772
  18.9 12.5 %copy-start.29 = (f32[64]{0:T(128)S(1)}, f32[64]{0:T(128)}, u32[]{:S(2)}) copy-start(f32[64]{0:T(128)} %copy-done.28) | copy-start | bytes 772
  18.9 12.5 %copy-start.32 = (f32[64]{0:T(128)S(1)}, f32[64]{0:T(128)}, u32[]{:S(2)}) copy-start(f32[64]{0:T(128)} %copy-done.31) | copy-start | bytes 772
  30.6 1.3 copy-start.24
  30.7 1.3 copy-start.37
  30.7 2.3 copy-start.17
  30.7 13.3 %copy-start.11 = (bf16[3,128,64]{1,2,0:T(8,128)(2,1)S(1)}, bf16[3,128,64]{1,2,0:T(8,128)(2,1)}, u32[]{:S(2)}) copy-start(bf16[3,128,64]{1,2,0:T(8,128)(2,1)} %param.13) | copy-start | bytes 147460
  33.0 12.3 %copy-start.6 = (f32[2,64,64]{2,1,0:T(8,128)}, f32[2,64,64]{2,1,0:T(8,128)S(1)}, u32[]{:S(2)}) copy-start(f32[2,64,64]{2,1,0:T(8,128)S(1)} %select_bitcast_fusion) | copy-start | bytes 98308
  45.3 0.8 copy-start.21
  45.3 0.8 copy-start.27
  45.3 0.8 copy-start.30
  45.3 0.8 copy-start.33
  46.5 5.2 collective-permute-start.1
  53.0 5.2 collective-permute-start.2
  55.4 3.4 copy-start.8
  62.2 3.8 collective-permute-start.3
  68.8 5.6 collective-permute-start.4
  75.8 5.9 copy-start.4
  75.8 53.4 %copy-start.2 = (bf16[64,4096]{1,0:T(8,128)(2,1)}, bf16[64,4096]{1,0:T(8,128)(2,1)S(1)}, u32[]{:S(2)}) copy-start(bf16[64,4096]{1,0:T(8,128)(2,1)S(1)} %get-tuple-element.13) | copy-start | bytes 1572868
  76.1 5.6 collective-permute-start.5
  81.0 1.4 copy-start.34
  111.5 25.8 %all-to-all-start = ((f32[8,1,1536]{2,1,0:T(1,128)}), f32[8,1,1536]{2,1,0:T(1,128)S(1)}, u32[]{:S(2)}, u32[]{:S(2)}) async-start(f32[8,1,1536]{2,1,0:T(1,128)} %reshape.486), calls=%async_computation | async-start | bytes 98304 | tf_op jit(solution)/shard_map/all_to_all | solution.py:138
  138.1 6.9 %copy-start.35 = (f32[8]{0:T(128)S(1)}, f32[8]{0:T(128)}, u32[]{:S(2)}) copy-start(f32[8]{0:T(128)} %get-tuple-element.42) | copy-start | bytes 100
  138.2 6.9 %copy-start.36 = (f32[8]{0:T(128)S(1)}, f32[8]{0:T(128)}, u32[]{:S(2)}) copy-start(f32[8]{0:T(128)} %get-tuple-element.43) | copy-start | bytes 100
  152.1 21.8 %copy-start.13 = (f32[3,8,1,512]{3,1,0,2:T(8,128)S(1)}, f32[3,8,1,512]{3,1,0,2:T(8,128)}, u32[]{:S(2)}) copy-start(f32[3,8,1,512]{3,1,0,2:T(8,128)} %get-tuple-element.25) | copy-start | bytes 147460
  154.6 24.7 %all-to-all-start.1 = ((f32[32,1,384]{2,1,0:T(1,128)}), f32[32,1,384]{2,1,0:T(1,128)S(1)}, u32[]{:S(2)}, u32[]{:S(2)}) async-start(f32[32,1,384]{2,1,0:T(1,128)} %reshape.488), calls=%async_computation.1 | async-start | bytes 98304 | tf_op jit(solution)/shard_map/all_to_all | solution.py:146
  179.3 14.1 %all-to-all-start.2 = ((f32[32,1,384]{2,1,0:T(1,128)}), f32[32,1,384]{2,1,0:T(1,128)S(1)}, u32[]{:S(2)}, u32[]{:S(2)}) async-start(f32[32,1,384]{2,1,0:T(1,128)} %reshape.490), calls=%async_computation.2 | async-start | bytes 98304 | tf_op jit(solution)/shard_map/all_to_all | solution.py:153
  196.4 22.2 %copy-start.1 = (bf16[64,4096]{1,0:T(8,128)(2,1)S(1)}, bf16[64,4096]{1,0:T(8,128)(2,1)}, u32[]{:S(2)}) copy-start(bf16[64,4096]{1,0:T(8,128)(2,1)} %copy-done) | copy-start | bytes 1572868
  196.4 22.2 %copy-start.3 = (bf16[64,4096]{1,0:T(8,128)(2,1)S(1)}, bf16[64,4096]{1,0:T(8,128)(2,1)}, u32[]{:S(2)}) copy-start(bf16[64,4096]{1,0:T(8,128)(2,1)} %copy-done.2) | copy-start | bytes 1572868
  196.4 22.2 %copy-start.5 = (bf16[64,4096]{1,0:T(8,128)(2,1)S(1)}, bf16[64,4096]{1,0:T(8,128)(2,1)}, u32[]{:S(2)}) copy-start(bf16[64,4096]{1,0:T(8,128)(2,1)} %copy-done.4) | copy-start | bytes 1572868
  201.5 12.2 %all-to-all-start.3 = ((f32[32,1,384]{2,1,0:T(1,128)}), f32[32,1,384]{2,1,0:T(1,128)S(1)}, u32[]{:S(2)}, u32[]{:S(2)}) async-start(f32[32,1,384]{2,1,0:T(1,128)} %reshape.492), calls=%async_computation.3 | async-start | bytes 98304 | tf_op jit(solution)/shard_map/all_to_all | solution.py:170
  213.7 11.3 %all-to-all-start.5 = ((f32[32,1,384]{2,1,0:T(1,128)}), f32[32,1,384]{2,1,0:T(1,128)S(1)}, u32[]{:S(2)}, u32[]{:S(2)}) async-start(f32[32,1,384]{2,1,0:T(1,128)} %reshape.494), calls=%async_computation.5 | async-start | bytes 98304 | tf_op jit(solution)/shard_map/all_to_all | solution.py:171
  218.6 9.7 %copy-start.19 = (f32[1,128,64]{1,2,0:T(8,128)S(1)}, f32[1,128,64]{1,2,0:T(8,128)}, u32[]{:S(2)}) copy-start(f32[1,128,64]{1,2,0:T(8,128)} %convolution_bitcast_fusion.11) | copy-start | bytes 98308
  218.7 9.7 %copy-start.20 = (f32[1,128,64]{1,2,0:T(8,128)S(1)}, f32[1,128,64]{1,2,0:T(8,128)}, u32[]{:S(2)}) copy-start(f32[1,128,64]{1,2,0:T(8,128)} %convolution_bitcast_fusion.12) | copy-start | bytes 98308
  225.0 11.7 %all-to-all-start.4 = ((f32[3,8,512]{2,0,1:T(4,128)}), f32[3,8,512]{2,0,1:T(4,128)S(1)}, u32[]{:S(2)}, u32[]{:S(2)}) async-start(f32[3,8,512]{2,0,1:T(4,128)} %reshape.475), calls=%async_computation.4 | async-start | bytes 131072 | tf_op jit(solution)/shard_map/all_to_all | solution.py:174
  228.3 312.2 %all-reduce.7.cloned.1.call-start = ((), (), s32[]{:S(2)}) async-start(), calls=%async_computation.14 | async-start | bytes 393216 | tf_op jit(solution)/shard_map/psum | solution.py:303
  229.1 21.0 %copy-start.7 = (f32[2,64,64]{2,1,0:T(8,128)S(1)}, f32[2,64,64]{2,1,0:T(8,128)}, u32[]{:S(2)}) copy-start(f32[2,64,64]{2,1,0:T(8,128)} %copy-done.6) | copy-start | bytes 98308
  229.1 21.0 %copy-start.9 = (f32[1,64,64]{2,1,0:T(8,128)S(1)}, f32[1,64,64]{2,1,0:T(8,128)}, u32[]{:S(2)}) copy-start(f32[1,64,64]{2,1,0:T(8,128)} %slice.152) | copy-start | bytes 49156
  236.6 11.8 %all-to-all-start.6 = ((f32[3,8,512]{2,0,1:T(4,128)}), f32[3,8,512]{2,0,1:T(4,128)S(1)}, u32[]{:S(2)}, u32[]{:S(2)}) async-start(f32[3,8,512]{2,0,1:T(4,128)} %reshape.476), calls=%async_computation.6 | async-start | bytes 131072 | tf_op jit(solution)/shard_map/all_to_all | solution.py:181
  250.1 4.3 copy-start.16
  276.3 7.3 %copy-start.14 = (f32[1,64,64]{2,1,0:T(8,128)S(1)}, f32[1,64,64]{2,1,0:T(8,128)}, u32[]{:S(2)}) copy-start(f32[1,64,64]{2,1,0:T(8,128)} %convolution_bitcast_fusion.18) | copy-start | bytes 49156
  276.3 7.3 %copy-start.15 = (f32[1,64,64]{2,1,0:T(8,128)S(1)}, f32[1,64,64]{2,1,0:T(8,128)}, u32[]{:S(2)}) copy-start(f32[1,64,64]{2,1,0:T(8,128)} %convolution_bitcast_fusion.19) | copy-start | bytes 49156
  276.3 7.3 %copy-start.18 = (f32[1,64,64]{2,1,0:T(8,128)S(1)}, f32[1,64,64]{2,1,0:T(8,128)}, u32[]{:S(2)}) copy-start(f32[1,64,64]{2,1,0:T(8,128)} %convolution_bitcast_fusion.17) | copy-start | bytes 49156
  280.1 29.2 %all-to-all-start.7 = ((f32[8,1,1536]{2,1,0:T(1,128)}), f32[8,1,1536]{2,1,0:T(1,128)S(1)}, u32[]{:S(2)}, u32[]{:S(2)}) async-start(f32[8,1,1536]{2,1,0:T(1,128)} %reshape.496), calls=%async_computation.7 | async-start | bytes 98304 | tf_op jit(solution)/shard_map/all_to_all | solution.py:196
  305.5 10.9 %copy-start.10 = (f32[3,4096]{1,0:T(4,128)S(1)}, f32[3,4096]{1,0:T(4,128)}, u32[]{:S(2)}) copy-start(f32[3,4096]{1,0:T(4,128)} %param.9) | copy-start | bytes 147460
  309.3 140.4 %all-to-all-start.9 = ((f32[8,1,1536]{2,1,0:T(1,128)}), f32[8,1,1536]{2,1,0:T(1,128)S(1)}, u32[]{:S(2)}, u32[]{:S(2)}) async-start(f32[8,1,1536]{2,1,0:T(1,128)} %reshape.500), calls=%async_computation.9 | async-start | bytes 98304 | tf_op jit(solution)/shard_map/all_to_all | solution.py:203
  449.7 53.5 %all-to-all-start.8 = ((f32[32,1,384]{2,1,0:T(1,128)}), f32[32,1,384]{2,1,0:T(1,128)S(1)}, u32[]{:S(2)}, u32[]{:S(2)}) async-start(f32[32,1,384]{2,1,0:T(1,128)} %reshape.498), calls=%async_computation.8 | async-start | bytes 98304 | tf_op jit(solution)/shard_map/all_to_all | solution.py:212
  503.2 13.9 %all-to-all-start.10 = ((f32[32,1,384]{2,1,0:T(1,128)}), f32[32,1,384]{2,1,0:T(1,128)S(1)}, u32[]{:S(2)}, u32[]{:S(2)}) async-start(f32[32,1,384]{2,1,0:T(1,128)} %reshape.502), calls=%async_computation.10 | async-start | bytes 98304 | tf_op jit(solution)/shard_map/all_to_all | solution.py:219
  514.0 6.9 %copy-start.22 = (f32[8,32]{1,0:T(8,128)S(1)}, f32[8,32]{1,0:T(8,128)}, u32[]{:S(2)}) copy-start(f32[8,32]{1,0:T(8,128)} %get-tuple-element.40) | copy-start | bytes 3076
  514.1 6.9 %copy-start.23 = (f32[8,32]{1,0:T(8,128)S(1)}, f32[8,32]{1,0:T(8,128)}, u32[]{:S(2)}) copy-start(f32[8,32]{1,0:T(8,128)} %get-tuple-element.41) | copy-start | bytes 3076
  522.8 12.2 %all-to-all-start.12 = ((f32[32,1,384]{2,1,0:T(1,128)}), f32[32,1,384]{2,1,0:T(1,128)S(1)}, u32[]{:S(2)}, u32[]{:S(2)}) async-start(f32[32,1,384]{2,1,0:T(1,128)} %reshape.506), calls=%async_computation.12 | async-start | bytes 98304 | tf_op jit(solution)/shard_map/all_to_all | solution.py:233
  535.0 11.3 %all-to-all-start.11 = ((f32[32,1,384]{2,1,0:T(1,128)}), f32[32,1,384]{2,1,0:T(1,128)S(1)}, u32[]{:S(2)}, u32[]{:S(2)}) async-start(f32[32,1,384]{2,1,0:T(1,128)} %reshape.504), calls=%async_computation.11 | async-start | bytes 98304 | tf_op jit(solution)/shard_map/all_to_all | solution.py:232
  540.0 74.8 %all-reduce.9.cloned.1.call-start = ((), (), s32[]{:S(2)}) async-start(), calls=%async_computation.15 | async-start | bytes 393216 | tf_op jit(solution)/shard_map/psum | solution.py:302
  548.7 67.6 %all-to-all-start.13 = ((f32[3,8,512]{2,0,1:T(4,128)}), f32[3,8,512]{2,0,1:T(4,128)S(1)}, u32[]{:S(2)}, u32[]{:S(2)}) async-start(f32[3,8,512]{2,0,1:T(4,128)} %copy.204), calls=%async_computation.13 | async-start | bytes 131072 | tf_op jit(solution)/shard_map/all_to_all | solution.py:241
Sparse Core Ops, SparseCore 0:
  233.1 109.6 all-reduce.6
  543.1 71.5 all-reduce.8
